TPU v7x, 1024 devices: a whole 4x8x16 slice. The times are simulated.
1024 devices in a mesh: ctx: 64 (over z, x_hi, core), head: 16 (over x_lo, y).
Axes of the slice: x: 4 (x_hi: 2, x_lo: 2; x = x_hi * 2 + x_lo), y: 8, z: 16, core: 2. Of those that a mesh axis runs over, the one named last changes fastest.
Arguments:
- tokens: bfloat16 [16384, 2048], P('ctx'), may hold values from -15 to 15
- w_qkv: bfloat16 [3, 2048, 2048], P(None, None, 'head'), may hold values from -0.9943689 to 0.9943689
- w_out: bfloat16 [2048, 2048], P('head'), may hold values from -0.125 to 0.125
- w_dec: bfloat16 [2048, 12, 256], P(None, None, 'head'), may hold values from -0.125 to 0.125
Outputs:
- field: float32 [16384, 8, 256], P('ctx', None, 'head')
All inputs are finite; a program needn't handle non-finite values.
Results may differ from a plain program's by a relative error of at most 0.011.
Values may be sent and summed in bfloat16 or wider, within the bound.
A program may use at most 32 MiB of HBM per device.

v0:
```python
import math

import jax
import jax.numpy as jnp
from jax import lax
from jax.sharding import PartitionSpec as P

HD = 64
PATCH = 8
OV = 2


eps = 1e-05


def passed_along(value, axis, steps):
    count = lax.axis_size(axis)
    pairs = [(source, (source + steps) % count) for source in range(count)]
    return lax.ppermute(value, axis, pairs)


def rms_scale(values):
    return values * lax.rsqrt(jnp.mean(values * values, axis=-1, keepdims=True) + eps)


def body(tokens, w_qkv, w_out, w_dec):
    rows = tokens.shape[0]
    local_heads = w_qkv.shape[2] // HD
    xf = tokens.astype(jnp.float32)
    normed = rms_scale(xf).astype(jnp.bfloat16)
    projected = jnp.einsum("td,kdc->ktc", normed, w_qkv, preferred_element_type=jnp.float32).astype(
        jnp.bfloat16
    )
    queries = projected[0].reshape(rows, local_heads, HD)
    keyvals = projected[1:]
    scale = HD ** (-0.5)

    def block_update(carry, block):
        best, total, accum = carry
        keys = block[0].reshape(-1, local_heads, HD)
        values = block[1].reshape(-1, local_heads, HD)
        scores = (
            jnp.einsum("thd,rhd->thr", queries, keys, preferred_element_type=jnp.float32) * scale
        )
        fresh = jnp.maximum(best, jnp.max(scores, axis=-1))
        shrink = jnp.exp(best - fresh)
        weights = jnp.exp(scores - fresh[..., None])
        total = total * shrink + jnp.sum(weights, axis=-1)
        accum = accum * shrink[..., None] + jnp.einsum(
            "thr,rhd->thd", weights.astype(jnp.bfloat16), values, preferred_element_type=jnp.float32
        )
        return (fresh, total, accum)

    initial = (
        jnp.full((rows, local_heads), -1e30, jnp.float32),
        jnp.zeros((rows, local_heads), jnp.float32),
        jnp.zeros((rows, local_heads, HD), jnp.float32),
    )
    piece = lax.all_gather(keyvals, "ctx", axis=1, tiled=True)
    length = piece.shape[1]
    span = math.gcd(length, 1024)

    def one_block(index, inner):
        block = lax.dynamic_slice_in_dim(piece, index * span, span, 1)
        return block_update(inner, block)

    best, total, accum = lax.fori_loop(0, length // span, one_block, initial)
    attended = (accum / total[..., None]).astype(jnp.bfloat16).reshape(rows, local_heads * HD)
    partial_out = jnp.dot(attended, w_out, preferred_element_type=jnp.float32)
    mixed = lax.psum(partial_out.astype(jnp.bfloat16), "head").astype(jnp.float32)
    hidden = rms_scale(xf + mixed).astype(jnp.bfloat16)
    extended = jnp.dot(
        hidden, w_dec.reshape(w_dec.shape[0], -1), preferred_element_type=jnp.float32
    )
    extended = extended.reshape(rows, w_dec.shape[1], w_dec.shape[2])
    from_before = passed_along(extended[:, PATCH + OV :].astype(jnp.bfloat16), "ctx", 1).astype(
        jnp.float32
    )
    from_after = passed_along(extended[:, :OV].astype(jnp.bfloat16), "ctx", -1).astype(jnp.float32)
    middle = extended[:, OV : OV + PATCH]
    field = jnp.concatenate(
        [
            middle[:, :OV] + from_before,
            middle[:, OV : PATCH - OV],
            middle[:, PATCH - OV :] + from_after,
        ],
        axis=1,
    )
    return field


def solution(mesh):
    return jax.shard_map(
        body,
        mesh=mesh,
        in_specs=(P("ctx", None), P(None, None, "head"), P("head", None), P(None, None, "head")),
        out_specs=P("ctx", None, "head"),
        check_vma=False,
    )
```

profile of v0, /device:TPU:1, one launch (start us, length us, event | category | flops | bytes accessed | tf_op | source)
XLA Modules:
  0.0 407.9 jit_solution(13003298857426968820)
XLA Ops:
  6.5 1.9 copy.6
  8.7 0.7 fusion.15
  9.4 0.7 slice.50
  10.2 187.0 %all-gather.2.cloned.1.call-done = bf16[2,16384,128]{1,2,0:T(8,128)(2,1)} async-done(((bf16[2,256,128]{1,2,0:T(8,128)(2,1)}), bf16[2,16384,128]{1,2,0:T(8,128)(2,1)}) %all-gather.2.cloned.1.call-update) | async-done | bytes 8388624 | tf_op jit(solution)/shard_map/all_gather | solution.py:59
  197.2 40.2 %while.18 = (s32[]{:T(128)}, f32[256,2]{0,1:T(2,128)S(1)}, f32[256,2]{0,1:T(2,128)S(1)}, f32[256,2,64]{0,2,1:T(8,128)S(1)}, bf16[2,16384,128]{1,2,0:T(8,128)(2,1...) while((s32[]{:T(128)}, f32[256,2]{0,1:T(2,128)S(1)}, ...), condition=%wide.region_4.0_spmd.clone, body=%wide.region_1.0_spmd.clone.sunk | while | flops 138512896 | bytes 8224955 | solution.py:67
  197.2 1.1 constant_dynamic-slice_fusion.3
  198.3 0.5 bitcast_reduce_fusion.2
  199.2 0.5 fusion.43
  199.7 1.1 constant_dynamic-slice_fusion.3
  200.8 0.5 bitcast_reduce_fusion.2
  202.2 1.1 constant_dynamic-slice_fusion.3
  203.3 0.5 bitcast_reduce_fusion.2
  204.8 1.1 constant_dynamic-slice_fusion.3
  205.8 0.5 bitcast_reduce_fusion.2
  207.3 1.1 constant_dynamic-slice_fusion.3
  208.4 0.5 bitcast_reduce_fusion.2
  209.8 1.1 constant_dynamic-slice_fusion.3
  210.9 0.5 bitcast_reduce_fusion.2
  212.3 1.1 constant_dynamic-slice_fusion.3
  213.4 0.5 bitcast_reduce_fusion.2
  214.8 1.1 constant_dynamic-slice_fusion.3
  215.9 0.5 bitcast_reduce_fusion.2
  216.8 0.5 fusion.43
  217.3 1.1 constant_dynamic-slice_fusion.3
  218.4 0.5 bitcast_reduce_fusion.2
  219.8 1.1 constant_dynamic-slice_fusion.3
  220.9 0.5 bitcast_reduce_fusion.2
  222.4 1.1 constant_dynamic-slice_fusion.3
  223.4 0.5 bitcast_reduce_fusion.2
  224.9 1.1 constant_dynamic-slice_fusion.3
  225.9 0.5 bitcast_reduce_fusion.2
  226.9 0.5 fusion.43
  227.4 1.1 constant_dynamic-slice_fusion.3
  228.5 0.5 bitcast_reduce_fusion.2
  229.9 1.1 constant_dynamic-slice_fusion.3
  231.0 0.5 bitcast_reduce_fusion.2
  232.4 1.1 constant_dynamic-slice_fusion.3
  233.5 0.5 bitcast_reduce_fusion.2
  234.9 1.1 constant_dynamic-slice_fusion.3
  236.0 0.5 bitcast_reduce_fusion.2
  237.5 2.6 convolution_convert_fusion
  240.1 135.4 %all-reduce.2.cloned.1.call-done = bf16[256,2048]{1,0:T(8,128)(2,1)} async-done(((bf16[256,2048]{1,0:T(8,128)(2,1)}), bf16[256,2048]{1,0:T(8,128)(2,1)}) %all-reduce.2.cloned.1.call-update) | async-done | bytes 1048592 | tf_op jit(solution)/shard_map/psum | solution.py:70
  375.5 1.7 multiply_reduce_fusion
  377.3 0.7 fusion.21
  378.0 15.9 %collective-permute-start = (bf16[256,2,16]{0,2,1:T(8,128)(2,1)S(1)}, bf16[256,2,16]{0,2,1:T(8,128)(2,1)S(1)}, u32[]{:S(2)}, u32[]{:S(2)}) collective-permute-start(bf16[256,2,16]{0,2,1:T(8,128)(2,1)S(1)} %get-tuple-element.158), channel_id=1, source_target_pairs={{0,16},{16,32},{32,48},{48,64},{64,80},{80,96},{96,112},{112,128},... | collective-permute-start | bytes 49160 | tf_op jit(solution)/shard_map/ppermute | solution.py:19
  393.9 1.9 collective-permute-start.1
  395.8 4.6 %collective-permute-done.1 = bf16[256,2,16]{0,2,1:T(8,128)(2,1)S(1)} collective-permute-done((bf16[256,2,16]{0,2,1:T(8,128)(2,1)S(1)}, bf16[256,2,16]{0,2,1:T(8,128)(2,1)S(1)}, u32[]{:S(2)}, u32[]{:S(2)}) %collective-permute-start.1) | collective-permute-done | bytes 16416 | tf_op jit(solution)/shard_map/ppermute | solution.py:19
  400.4 0.7 pad_maximum_fusion
  (102 shorter events, 13.1 us)
Async XLA Ops:
  6.5 370.7 %copy-start = (bf16[2048,12,16]{0,2,1:T(8,128)(2,1)S(1)}, bf16[2048,12,16]{0,2,1:T(8,128)(2,1)}, u32[]{:S(2)}) copy-start(bf16[2048,12,16]{0,2,1:T(8,128)(2,1)} %param.9) | copy-start | bytes 2359300
  6.5 1.9 copy-start.1
  6.5 190.7 %all-gather.2.cloned.1.call-start = ((), (), s32[]{:S(2)}) async-start(), calls=%async_computation | async-start | bytes 8519680 | tf_op jit(solution)/shard_map/all_gather | solution.py:59
  10.1 365.4 %all-reduce.2.cloned.1.call-start = ((), (), s32[]{:S(2)}) async-start(), calls=%async_computation.1 | async-start | bytes 2097152 | tf_op jit(solution)/shard_map/psum | solution.py:70
  237.4 138.1 %copy-start.2 = (bf16[256,2048]{1,0:T(8,128)(2,1)S(1)}, bf16[256,2048]{1,0:T(8,128)(2,1)}, u32[]{:S(2)}) copy-start(bf16[256,2048]{1,0:T(8,128)(2,1)} %param.6) | copy-start | bytes 3145732
  375.5 1.8 copy-start.3
  378.0 17.9 %collective-permute-start = (bf16[256,2,16]{0,2,1:T(8,128)(2,1)S(1)}, bf16[256,2,16]{0,2,1:T(8,128)(2,1)S(1)}, u32[]{:S(2)}, u32[]{:S(2)}) collective-permute-start(bf16[256,2,16]{0,2,1:T(8,128)(2,1)S(1)} %get-tuple-element.158), channel_id=1, source_target_pairs={{0,16},{16,32},{32,48},{48,64},{64,80},{80,96},{96,112},{112,128},... | collective-permute-start | bytes 49160 | tf_op jit(solution)/shard_map/ppermute | solution.py:19
  393.9 6.6 %collective-permute-start.1 = (bf16[256,2,16]{0,2,1:T(8,128)(2,1)S(1)}, bf16[256,2,16]{0,2,1:T(8,128)(2,1)S(1)}, u32[]{:S(2)}, u32[]{:S(2)}) collective-permute-start(bf16[256,2,16]{0,2,1:T(8,128)(2,1)S(1)} %get-tuple-element.159), channel_id=1, source_target_pairs={{0,1008},{16,0},{32,16},{48,32},{64,48},{80,64},{96,80},{112,96},{... | collective-permute-start | bytes 49160 | tf_op jit(solution)/shard_map/ppermute | solution.py:19
Sparse Core Ops, SparseCore 0:
  11.5 185.6 all-gather.1
  240.2 135.2 all-reduce.1
where the time goes:
time: 408 us
  waiting for transfers between devices  327 us (80%)
  matrix products  19.9 us (5%)
  local copies, waits for them, and re-layouts  19.7 us (5%)
  starting transfers between devices  17.9 us (4%)
  between operations  13.6 us (3%)
  other arithmetic  8.94 us (2%)
    all_gather x1, waiting for transfers between devices, body(): piece = lax.all_gather(keyvals, 'ctx', axis=1, tiled=True)  187 us
    psum x1, waiting for transfers between devices, body(): lax.psum(partial_out.astype(jnp.bfloat16), 'head').astype(jnp.float32)  135 us
    ppermute x2, starting transfers between devices, passed_along(): return lax.ppermute(value, axis, pairs)  17.8 us
    slice x16, local copies, waits for them, and re-layouts, block_update(): values = block[1].reshape(-1, local_heads, HD)  17.1 us
  transfers between devices with their start and end apart: 4, of which 3 were waited for; matrix products, arithmetic and copies ran while one was open for 0% of the time, Pallas kernels for 0%

commit v1 on v0

v1 whole, which is shorter than its diff:
```python
import functools

import jax
import jax.numpy as jnp
from jax import lax
from jax.experimental import pallas as pl
from jax.experimental.pallas import tpu as pltpu
from jax.sharding import PartitionSpec as P

HD = 64
PATCH = 8
OV = 2
EPS = 1e-05
LOG2E = 1.4426950408889634
F32 = jnp.float32
BF16 = jnp.bfloat16


def nt(a, b):
    return lax.dot_general(a, b, (((1,), (1,)), ((), ())), preferred_element_type=F32)


def nn(a, b):
    return jnp.dot(a, b, preferred_element_type=F32)


def kernel(
    n_ctx,
    n_head,
    tok_hbm,
    wqkv_hbm,
    wout_hbm,
    wdec_hbm,
    out_ref,
    tok,
    wqkv,
    wout,
    wdec,
    wout_t,
    wcol_t,
    q_raw,
    q_pad,
    kbuf,
    vbuf,
    m_ref,
    l_ref,
    acc,
    part_send,
    stat_send,
    part_recv,
    stat_recv,
    att,
    hid,
    halo_send,
    halo_recv,
    load_sem,
    own_send,
    k_send,
    v_send,
    k_recv,
    v_recv,
    q_send,
    q_recv,
    w_send,
    w_recv,
    c_send,
    c_recv,
    st_send,
    st_recv,
    g_recv,
    g_pos,
    g_neg,
    g_pair,
    halo_ssem,
    halo_rsem,
):
    rows, width = tok.shape
    nz, ny = n_ctx // 4, n_head // 2
    last = nz - 1
    cols = 2 * HD
    cells = PATCH * 16

    ctx = lax.axis_index("ctx")
    head = lax.axis_index("head")
    core = ctx % 2
    xh = (ctx // 2) % 2
    z = ctx // 4
    xl = head // ny
    y = head % ny
    mine = xh * 2 + core
    up = (z + 1) % nz
    down = (z + nz - 1) % nz
    dev_up = (up * 4 + xh * 2, head)
    dev_down = (down * 4 + xh * 2 + 1, head)

    def remote(src, dst, ssem, rsem, device):
        return pltpu.make_async_remote_copy(
            src_ref=src,
            dst_ref=dst,
            send_sem=ssem,
            recv_sem=rsem,
            device_id=device,
            device_id_type=pl.DeviceIdType.MESH,
        )

    loads = [
        pltpu.make_async_copy(a, b, load_sem.at[i])
        for i, (a, b) in enumerate(
            ((tok_hbm, tok), (wqkv_hbm, wqkv), (wout_hbm, wout), (wdec_hbm, wdec))
        )
    ]
    for load in loads:
        load.start()

    barrier = pltpu.get_barrier_semaphore()

    def greet(device):
        pl.semaphore_signal(
            barrier, inc=1, device_id=device, device_id_type=pl.DeviceIdType.MESH
        )

    source_z = (z + nz - 1 + 2 * core) % nz
    greet((source_z * 4 + xh * 2, head))
    greet((source_z * 4 + xh * 2 + 1, head))
    for step in range(1, 4):
        other = (mine + step) % 4
        greet((z * 4 + other, head))

    @pl.loop(1, n_head)
    def _(step):
        greet((ctx, (head + step) % n_head))

    greet(((ctx + 1) % n_ctx, head))
    greet(((ctx + n_ctx - 1) % n_ctx, head))

    loads[0].wait()
    x = tok[...]
    xf = x.astype(F32)
    r = lax.rsqrt(jnp.mean(xf * xf, axis=-1, keepdims=True) + EPS)
    loads[1].wait()
    kbuf[0] = (nn(x, wqkv[1]) * r).astype(BF16)
    vbuf[0] = (nn(x, wqkv[2]) * r).T.astype(BF16)
    pl.semaphore_wait(barrier, n_head + 6)

    first = []
    for t, device in enumerate((dev_up, dev_down)):
        first.append(
            remote(kbuf.at[0], kbuf.at[1 + core], own_send.at[2 * t], k_recv.at[1 + core], device)
        )
        first.append(
            remote(
                vbuf.at[0], vbuf.at[1 + core], own_send.at[2 * t + 1], v_recv.at[1 + core], device
            )
        )
    for copy in first:
        copy.start()

    q_raw[mine] = (nn(x, wqkv[0]) * (r * (HD**-0.5 * LOG2E))).astype(BF16)
    q_copies = []
    for step in (2, 1, 3):
        other = (mine + step) % 4
        q_copies.append(
            remote(
                q_raw.at[mine], q_raw.at[mine], q_send.at[step], q_recv.at[mine], (z * 4 + other, head)
            )
        )
    for copy in q_copies:
        copy.start()

    def forward(j, buf, ssem, rsem):
        target = jnp.minimum(j + 2, last)
        return remote(
            buf.at[j],
            buf.at[target],
            ssem.at[j],
            rsem.at[target],
            ((z + 1 + core * (nz - 2)) % nz * 4 + xh * 2 + core, head),
        )

    def passes_on(j):
        return jnp.logical_or(j <= last - 3, j == last - 2 + core)

    def arrive(j):
        for buf, ssem, rsem in ((kbuf, k_send, k_recv), (vbuf, v_send, v_recv)):
            remote(buf.at[j], buf.at[j], ssem.at[j], rsem.at[j], dev_up).wait_recv()

            @pl.when(passes_on(j))
            def _():
                forward(j, buf, ssem, rsem).start()

    loads[2].wait()
    wout_t[...] = wout[...].astype(F32).T.astype(BF16)
    wcol_t[head] = wout_t[pl.ds(pl.multiple_of(head * cols, cols), cols), :]

    def w_copy(step):
        other = (head + step) % n_head
        return remote(
            wout_t.at[pl.ds(pl.multiple_of(other * cols, cols), cols), :],
            wcol_t.at[head],
            w_send.at[step],
            w_recv.at[head],
            (ctx, other),
        )

    @pl.loop(1, n_head)
    def _(step):
        w_copy(step).start()

    arrive(1)

    m_ref[...] = jnp.full_like(m_ref, -1e30)
    l_ref[...] = jnp.zeros_like(l_ref)
    acc[...] = jnp.zeros_like(acc)
    for step in range(1, 4):
        other = (mine + step) % 4
        remote(
            q_raw.at[other], q_raw.at[other], q_send.at[step], q_recv.at[other], dev_up
        ).wait_recv()
    low = lax.broadcasted_iota(jnp.int32, (rows, cols), 1) < HD
    for b in range(4):
        q = q_raw[b]
        zero = jnp.zeros_like(q)
        q_pad[0, b * rows : (b + 1) * rows, :] = jnp.where(low, q, zero)
        q_pad[1, b * rows : (b + 1) * rows, :] = jnp.where(low, zero, q)

    def attend(j):
        keys = kbuf[j]
        values = vbuf[j]
        for h in range(2):
            for part in range(2):
                span = slice(part * 2 * rows, (part + 1) * 2 * rows)
                scores = nt(keys, q_pad[h, span, :])
                old = m_ref[h : h + 1, span]
                new = jnp.maximum(old, jnp.max(scores, axis=0, keepdims=True))
                weights = jnp.exp2(scores - new)
                shrink = jnp.exp2(old - new)
                m_ref[h : h + 1, span] = new
                l_ref[h : h + 1, span] = l_ref[h : h + 1, span] * shrink + jnp.sum(
                    weights, axis=0, keepdims=True
                )
                acc[h, :, span] = acc[h, :, span] * shrink + nn(
                    values[h * HD : (h + 1) * HD, :], weights.astype(BF16)
                )

    @pl.loop(1, nz + 1)
    def _(j):
        @pl.when(jnp.logical_and(j >= 2, j <= last))
        def _():
            arrive(j)

        attend(j - 1)

    c_copies = []
    for step in (2, 1, 3):
        other = (mine + step) % 4
        span = pl.ds(pl.multiple_of(other * rows, rows), rows)
        for h in range(2):
            part_send[other, h * HD : (h + 1) * HD, :] = acc[h, :, span].astype(BF16)
            stat_send[other, h : h + 1, :] = m_ref[h : h + 1, span]
            stat_send[other, 2 + h : 3 + h, :] = l_ref[h : h + 1, span]
        device = (z * 4 + other, head)
        c_copies.append(
            remote(part_send.at[other], part_recv.at[mine], c_send.at[step], c_recv.at[mine], device)
        )
        c_copies.append(
            remote(
                stat_send.at[other], stat_recv.at[mine], st_send.at[step], st_recv.at[mine], device
            )
        )
        c_copies[-2].start()
        c_copies[-1].start()

    @pl.loop(1, last)
    def _(j):
        @pl.when(passes_on(j))
        def _():
            forward(j, kbuf, k_send, k_recv).wait_send()
            forward(j, vbuf, v_send, v_recv).wait_send()

    for copy in first + q_copies:
        copy.wait_send()

    for step in range(1, 4):
        other = (mine + step) % 4
        remote(
            part_recv.at[other], part_recv.at[other], c_send.at[step], c_recv.at[other], dev_up
        ).wait_recv()
        remote(
            stat_recv.at[other], stat_recv.at[other], st_send.at[step], st_recv.at[other], dev_up
        ).wait_recv()
    span = pl.ds(pl.multiple_of(mine * rows, rows), rows)
    for h in range(2):
        tops = [m_ref[h : h + 1, span]]
        sums = [l_ref[h : h + 1, span]]
        parts = [acc[h, :, span]]
        for step in range(1, 4):
            other = (mine + step) % 4
            tops.append(stat_recv[other, h : h + 1, :])
            sums.append(stat_recv[other, 2 + h : 3 + h, :])
            parts.append(part_recv[other, h * HD : (h + 1) * HD, :].astype(F32))
        top = functools.reduce(jnp.maximum, tops)
        scales = [jnp.exp2(t - top) for t in tops]
        total = functools.reduce(jnp.add, [a * b for a, b in zip(scales, sums)])
        inverse = 1.0 / total
        mixed = functools.reduce(jnp.add, [(a * inverse) * b for a, b in zip(scales, parts)])
        att[head, h * HD : (h + 1) * HD, :] = mixed.astype(BF16)

    sign = 1 - 2 * core
    pair = (ctx, (1 - xl) * ny + y)
    pos = (ctx, xl * ny + (y + sign + ny) % ny)
    neg = (ctx, xl * ny + (y - sign + ny) % ny)

    def gather(which, buf, use):
        started = []

        def send(src, sems, device):
            copy = remote(
                buf.at[src], buf.at[src], sems.at[which, src], g_recv.at[which, src], device
            )
            copy.start()
            started.append(copy)

        def wait(src):
            remote(
                buf.at[src], buf.at[src], g_pos.at[which, src], g_recv.at[which, src], pos
            ).wait_recv()

        send(head, g_pair, pair)
        send(head, g_pos, pos)
        send(head, g_neg, neg)
        use(head)
        src = (1 - xl) * ny + y
        wait(src)
        send(src, g_pos, pos)
        use(src)
        half = ny // 2
        for d in range(1, half + 1):
            behind = (y - sign * d + ny) % ny
            ahead = (y + sign * d + ny) % ny
            if d < half:
                src = xl * ny + behind
                wait(src)
                if d < half - 1:
                    send(src, g_pos, pos)
            ahead_src = xl * ny + ahead
            wait(ahead_src)
            send(ahead_src, g_pair, pair)
            if d < half:
                send(ahead_src, g_neg, neg)
                use(src)
                far = (1 - xl) * ny + behind
                wait(far)
                if d < half - 1:
                    send(far, g_pos, pos)
                use(far)
            use(ahead_src)
            far = (1 - xl) * ny + ahead
            wait(far)
            use(far)
        return started

    residual = tok[:, pl.ds(pl.multiple_of(head * cols, cols), cols)].astype(F32).T

    @pl.loop(1, n_head)
    def _(step):
        other = (head + step) % n_head
        remote(
            wcol_t.at[other], wcol_t.at[other], w_send.at[step], w_recv.at[other], pos
        ).wait_recv()

    total = [residual]

    def project(src):
        total[0] = total[0] + nn(wcol_t[src], att[src])

    started = gather(0, att, project)
    hid[head] = total[0].astype(BF16)

    ext = [jnp.zeros((wdec.shape[0], rows), F32)]
    squares = [jnp.zeros((cols, rows), F32)]

    def decode(src):
        block = hid[src]
        wide = block.astype(F32)
        squares[0] = squares[0] + wide * wide
        ext[0] = ext[0] + nn(wdec[:, pl.ds(pl.multiple_of(src * cols, cols), cols)], block)

    loads[3].wait()
    started += gather(1, hid, decode)
    mean = jnp.sum(squares[0], axis=0, keepdims=True) * (1.0 / width)
    field = ext[0] * lax.rsqrt(mean + EPS)

    edge = OV * 16
    halo_send[0] = field[cells + edge :, :].astype(BF16)
    halo_send[1] = field[:edge, :].astype(BF16)
    halos = []
    for i, device in enumerate((((ctx + 1) % n_ctx, head), ((ctx + n_ctx - 1) % n_ctx, head))):
        halos.append(
            remote(halo_send.at[i], halo_recv.at[i], halo_ssem.at[i], halo_rsem.at[i], device)
        )
    for copy in halos:
        copy.start()
    out_ref[edge : cells - edge, :] = field[2 * edge : cells, :]
    for copy in started + c_copies:
        copy.wait_send()

    @pl.loop(1, n_head)
    def _(step):
        w_copy(step).wait_send()

    halos[0].wait()
    out_ref[:edge, :] = field[edge : 2 * edge, :] + halo_recv[0].astype(F32)
    halos[1].wait()
    out_ref[cells - edge :, :] = field[cells : cells + edge, :] + halo_recv[1].astype(F32)


def body(n_ctx, n_head, tokens, w_qkv, w_out, w_dec):
    rows, width = tokens.shape
    cols = w_qkv.shape[2]
    nz = n_ctx // 4
    wdec_t = jnp.transpose(w_dec, (1, 2, 0)).reshape(-1, width)
    cells = PATCH * w_dec.shape[2]
    dma = pltpu.SemaphoreType.DMA
    anywhere = pl.BlockSpec(memory_space=pl.ANY)
    flops = 2 * rows * width * (3 * cols + cols + wdec_t.shape[0])
    flops += 4 * (4 * rows) * (rows * nz) * cols
    out = pl.pallas_call(
        functools.partial(kernel, n_ctx, n_head),
        out_shape=jax.ShapeDtypeStruct((cells, rows), F32),
        in_specs=[anywhere] * 4,
        out_specs=pl.BlockSpec(memory_space=pltpu.VMEM),
        scratch_shapes=[
            pltpu.VMEM((rows, width), BF16),
            pltpu.VMEM(w_qkv.shape, BF16),
            pltpu.VMEM(w_out.shape, BF16),
            pltpu.VMEM(wdec_t.shape, BF16),
            pltpu.VMEM((width, cols), BF16),
            pltpu.VMEM((n_head, cols, cols), BF16),
            pltpu.VMEM((4, rows, cols), BF16),
            pltpu.VMEM((2, 4 * rows, cols), BF16),
            pltpu.VMEM((nz, rows, cols), BF16),
            pltpu.VMEM((nz, cols, rows), BF16),
            pltpu.VMEM((2, 4 * rows), F32),
            pltpu.VMEM((2, 4 * rows), F32),
            pltpu.VMEM((2, HD, 4 * rows), F32),
            pltpu.VMEM((4, cols, rows), BF16),
            pltpu.VMEM((4, 8, rows), F32),
            pltpu.VMEM((4, cols, rows), BF16),
            pltpu.VMEM((4, 8, rows), F32),
            pltpu.VMEM((n_head, cols, rows), BF16),
            pltpu.VMEM((n_head, cols, rows), BF16),
            pltpu.VMEM((2, 2 * OV * 8, rows), BF16),
            pltpu.VMEM((2, 2 * OV * 8, rows), BF16),
            dma((4,)),
            dma((4,)),
            dma((nz,)),
            dma((nz,)),
            dma((nz,)),
            dma((nz,)),
            dma((4,)),
            dma((4,)),
            dma((n_head,)),
            dma((n_head,)),
            dma((4,)),
            dma((4,)),
            dma((4,)),
            dma((4,)),
            dma((2, n_head)),
            dma((2, n_head)),
            dma((2, n_head)),
            dma((2, n_head)),
            dma((2,)),
            dma((2,)),
        ],
        compiler_params=pltpu.CompilerParams(
            collective_id=0, has_side_effects=True, vmem_limit_bytes=48 * 1024 * 1024
        ),
        cost_estimate=pl.CostEstimate(flops=flops, bytes_accessed=1 << 22, transcendentals=1 << 23),
        name="layer",
    )(tokens, w_qkv, w_out, wdec_t)
    return jnp.transpose(out.reshape(PATCH, w_dec.shape[2], rows), (2, 0, 1))


def solution(mesh):
    return jax.shard_map(
        functools.partial(body, mesh.shape["ctx"], mesh.shape["head"]),
        mesh=mesh,
        in_specs=(P("ctx", None), P(None, None, "head"), P("head", None), P(None, None, "head")),
        out_specs=P("ctx", None, "head"),
        check_vma=False,
    )
```

time: 408 us -> 117 us (0.29)
  waiting for transfers between devices: 327 us -> 0 us
  Pallas kernels: 0 us -> 111 us
  matrix products: 19.9 us -> 0 us
  starting transfers between devices: 17.9 us -> 0 us
  local copies, waits for them, and re-layouts: 19.7 us -> 5.46 us
  between operations: 13.6 us -> 0.01 us
  other arithmetic: 8.94 us -> 0 us
    all_gather x1 -> x0, waiting for transfers between devices: 187 us -> none  [body(): piece = lax.all_gather(keyvals, 'ctx', axis=1, tiled=True)]
    psum x1 -> x0, waiting for transfers between devices: 135 us -> none  [body(): lax.psum(partial_out.astype(jnp.bfloat16), 'head').astype(jnp.float32)]
    pallas_call x0 -> x1, Pallas kernels: none -> 111 us  [body(): pl.pallas_call(functools.partial(kernel, n_ctx, n_head), out_shape=jax.Sh...]
    dot_general x34 -> x0, matrix products: 19.2 us -> none  [the longest x16 8.06 us: block_update(): jnp.einsum('thd,rhd->thr', queries, keys, preferred_element_type=jnp.floa...]
    ppermute x2 -> x0, starting transfers between devices: 17.8 us -> none  [passed_along(): return lax.ppermute(value, axis, pairs)]
    slice x20 -> x0, local copies, waits for them, and re-layouts: 17.8 us -> none  [the longest x16 17.1 us: block_update(): values = block[1].reshape(-1, local_heads, HD)]
    reduce_sum x18 -> x0, other arithmetic: 7.8 us -> none  [the longest x16 5.79 us: block_update(): total = total * shrink + jnp.sum(weights, axis=-1)]
    ppermute x2 -> x0, waiting for transfers between devices: 4.61 us -> none  [passed_along(): return lax.ppermute(value, axis, pairs)]
  transfers between devices with their start and end apart: 4 -> 0, of which waited for: 3 -> 0; matrix products, arithmetic and copies ran while one was open for 0% -> 0% of each run, Pallas kernels for 0% -> 0%
where the time goes in v1:
time: 117 us; the launch traced here: 116 us
  Pallas kernels  111 us (95%)
  local copies, waits for them, and re-layouts  5.46 us (5%)
    pallas_call x1, Pallas kernels, body(): pl.pallas_call(functools.partial(kernel, n_ctx, n_head), out_shape=jax.Sh...  111 us
    unnamed x9, local copies, waits for them, and re-layouts  5.46 us

profile of v1, /device:TPU:1, one launch (start us, length us, event | category | flops | bytes accessed | tf_op | source)
XLA Modules:
  0.0 116.4 jit_solution(3756886981790739461)
XLA Ops:
  0.0 0.0 copy-start
  0.0 1.4 %copy-done = bf16[3,2048,128]{2,1,0:T(8,128)(2,1)S(1)} copy-done((bf16[3,2048,128]{2,1,0:T(8,128)(2,1)S(1)}, bf16[3,2048,128]{2,1,0:T(8,128)(2,1)}, u32[]{:S(2)}) %copy-start) | copy-done | bytes 1572888
  1.4 0.0 copy-start.1
  1.4 1.2 %copy-done.1 = bf16[256,2048]{1,0:T(8,128)(2,1)S(1)} copy-done((bf16[256,2048]{1,0:T(8,128)(2,1)S(1)}, bf16[256,2048]{1,0:T(8,128)(2,1)}, u32[]{:S(2)}) %copy-start.1) | copy-done | bytes 1048600
  2.6 0.0 copy-start.2
  2.6 1.1 copy-done.2
  3.8 0.0 copy-start.3
  3.8 1.0 copy-done.3
  4.8 110.9 %layer.1 = f32[128,256]{1,0:T(8,128)S(1)} custom-call(bf16[256,2048]{1,0:T(8,128)(2,1)S(1)} %copy-done.1, bf16[3,2048,128]{2,1,0:T(8,128)(2,1)S(1)} %copy-done, bf16[128,2048]{1,0:T(8,128)(2,1)S(1)} %copy-done.3, bf16[192,2048]{1,0:T(8,128)(2,1)S(1)} %bitcast.7), custom_call_target="tpu_custom_call" | custom-call | flops 2885681152 | bytes 4194304 | tf_op jit(solution)/shard_map/layer/pallas_call | solution.py:427
  115.8 0.7 copy.6
Async XLA Ops:
  0.0 1.4 %copy-start = (bf16[3,2048,128]{2,1,0:T(8,128)(2,1)S(1)}, bf16[3,2048,128]{2,1,0:T(8,128)(2,1)}, u32[]{:S(2)}) copy-start(bf16[3,2048,128]{2,1,0:T(8,128)(2,1)} %wqkv_hbm.1) | copy-start | bytes 4718596
  1.4 1.2 %copy-start.1 = (bf16[256,2048]{1,0:T(8,128)(2,1)S(1)}, bf16[256,2048]{1,0:T(8,128)(2,1)}, u32[]{:S(2)}) copy-start(bf16[256,2048]{1,0:T(8,128)(2,1)} %tok_hbm.1) | copy-start | bytes 3145732
  2.6 1.1 copy-start.2
  3.8 1.0 copy-start.3

commit v2 on v1

--- a/solution.py
+++ b/solution.py
@@ -70,6 +70,8 @@
     g_recv,
     g_pos,
     g_neg,
+    g_pos2,
+    g_neg2,
     g_pair,
     halo_ssem,
     halo_rsem,
@@ -134,12 +136,13 @@
     greet(((ctx + n_ctx - 1) % n_ctx, head))
 
     loads[0].wait()
+    loads[1].wait()
     x = tok[...]
     xf = x.astype(F32)
     r = lax.rsqrt(jnp.mean(xf * xf, axis=-1, keepdims=True) + EPS)
-    loads[1].wait()
-    kbuf[0] = (nn(x, wqkv[1]) * r).astype(BF16)
-    vbuf[0] = (nn(x, wqkv[2]) * r).T.astype(BF16)
+    keyvals = nn(x, jnp.concatenate([wqkv[1], wqkv[2]], axis=1)) * r
+    kbuf[0] = keyvals[:, :cols].astype(BF16)
+    vbuf[0] = keyvals[:, cols:].T.astype(BF16)
     pl.semaphore_wait(barrier, n_head + 6)
 
     first = []
@@ -180,13 +183,14 @@
     def passes_on(j):
         return jnp.logical_or(j <= last - 3, j == last - 2 + core)
 
-    def arrive(j):
-        for buf, ssem, rsem in ((kbuf, k_send, k_recv), (vbuf, v_send, v_recv)):
-            remote(buf.at[j], buf.at[j], ssem.at[j], rsem.at[j], dev_up).wait_recv()
-
-            @pl.when(passes_on(j))
-            def _():
-                forward(j, buf, ssem, rsem).start()
+    def arrive(j, buf, ssem, rsem):
+        remote(buf.at[j], buf.at[j], ssem.at[j], rsem.at[j], dev_up).wait_recv()
+
+        @pl.when(passes_on(j))
+        def _():
+            forward(j, buf, ssem, rsem).start()
+
+    ring = ((kbuf, k_send, k_recv), (vbuf, v_send, v_recv))
 
     loads[2].wait()
     wout_t[...] = wout[...].astype(F32).T.astype(BF16)
@@ -201,12 +205,6 @@
             w_recv.at[head],
             (ctx, other),
         )
-
-    @pl.loop(1, n_head)
-    def _(step):
-        w_copy(step).start()
-
-    arrive(1)
 
     m_ref[...] = jnp.full_like(m_ref, -1e30)
     l_ref[...] = jnp.zeros_like(l_ref)
@@ -223,32 +221,46 @@
         q_pad[0, b * rows : (b + 1) * rows, :] = jnp.where(low, q, zero)
         q_pad[1, b * rows : (b + 1) * rows, :] = jnp.where(low, zero, q)
 
-    def attend(j):
-        keys = kbuf[j]
-        values = vbuf[j]
-        for h in range(2):
-            for part in range(2):
-                span = slice(part * 2 * rows, (part + 1) * 2 * rows)
-                scores = nt(keys, q_pad[h, span, :])
-                old = m_ref[h : h + 1, span]
-                new = jnp.maximum(old, jnp.max(scores, axis=0, keepdims=True))
-                weights = jnp.exp2(scores - new)
-                shrink = jnp.exp2(old - new)
-                m_ref[h : h + 1, span] = new
-                l_ref[h : h + 1, span] = l_ref[h : h + 1, span] * shrink + jnp.sum(
-                    weights, axis=0, keepdims=True
-                )
-                acc[h, :, span] = acc[h, :, span] * shrink + nn(
-                    values[h * HD : (h + 1) * HD, :], weights.astype(BF16)
-                )
-
-    @pl.loop(1, nz + 1)
-    def _(j):
-        @pl.when(jnp.logical_and(j >= 2, j <= last))
-        def _():
-            arrive(j)
-
-        attend(j - 1)
+    def attend(items, h, part):
+        span = slice(part * 2 * rows, (part + 1) * 2 * rows)
+        queries = q_pad[h, span, :]
+        scores = [nt(kbuf[j], queries) for j in items]
+        old = m_ref[h : h + 1, span]
+        new = old
+        for block in scores:
+            new = jnp.maximum(new, jnp.max(block, axis=0, keepdims=True))
+        weights = [jnp.exp2(block - new) for block in scores]
+        shrink = jnp.exp2(old - new)
+        m_ref[h : h + 1, span] = new
+        total = l_ref[h : h + 1, span] * shrink
+        summed = acc[h, :, span] * shrink
+        for j, block in zip(items, weights):
+            total = total + jnp.sum(block, axis=0, keepdims=True)
+            summed = summed + nn(vbuf[j, h * HD : (h + 1) * HD, :], block.astype(BF16))
+        l_ref[h : h + 1, span] = total
+        acc[h, :, span] = summed
+
+    for i in range(4):
+        arrive(1 + i // 2, *ring[i % 2])
+        attend((0,), i // 2, i % 2)
+    w_copy(last).start()
+
+    @pl.loop(1, nz // 2)
+    def _(hop):
+        first_item = 2 * hop - 1
+        w_copy(first_item).start()
+        w_copy(first_item + 1).start()
+        for i in range(4):
+            j = first_item + 2 + i // 2
+
+            @pl.when(j <= last)
+            def _():
+                arrive(j, *ring[i % 2])
+
+            attend((first_item, first_item + 1), i // 2, i % 2)
+
+    for i in range(4):
+        attend((last,), i // 2, i % 2)
 
     c_copies = []
     for step in (2, 1, 3):
@@ -306,57 +318,66 @@
         att[head, h * HD : (h + 1) * HD, :] = mixed.astype(BF16)
 
     sign = 1 - 2 * core
-    pair = (ctx, (1 - xl) * ny + y)
-    pos = (ctx, xl * ny + (y + sign + ny) % ny)
-    neg = (ctx, xl * ny + (y - sign + ny) % ny)
+
+    def along(side, steps):
+        return side * ny + (y + sign * steps + ny) % ny
+
+    other_side = 1 - xl
+    pair = (ctx, along(other_side, 0))
+    pos, pos2 = (ctx, along(xl, 1)), (ctx, along(xl, 2))
+    neg, neg2 = (ctx, along(xl, -1)), (ctx, along(xl, -2))
 
     def gather(which, buf, use):
         started = []
 
-        def send(src, sems, device):
-            copy = remote(
-                buf.at[src], buf.at[src], sems.at[which, src], g_recv.at[which, src], device
-            )
-            copy.start()
-            started.append(copy)
+        def send(src, *routes):
+            for sems, device in routes:
+                copy = remote(
+                    buf.at[src], buf.at[src], sems.at[which, src], g_recv.at[which, src], device
+                )
+                copy.start()
+                started.append(copy)
 
         def wait(src):
             remote(
                 buf.at[src], buf.at[src], g_pos.at[which, src], g_recv.at[which, src], pos
             ).wait_recv()
 
-        send(head, g_pair, pair)
-        send(head, g_pos, pos)
-        send(head, g_neg, neg)
+        to_pair = (g_pair, pair)
+        to_pos, to_pos2 = (g_pos, pos), (g_pos2, pos2)
+        to_neg, to_neg2 = (g_neg, neg), (g_neg2, neg2)
+        send(head, to_pair, to_pos2, to_neg2, to_pos, to_neg)
+        mate = along(other_side, 0)
+        ahead = [along(xl, d) for d in range(1, 5)]
+        behind = [along(xl, -d) for d in range(1, 4)]
+        far_ahead = [along(other_side, d) for d in range(1, 5)]
+        far_behind = [along(other_side, -d) for d in range(1, 4)]
         use(head)
-        src = (1 - xl) * ny + y
-        wait(src)
-        send(src, g_pos, pos)
-        use(src)
-        half = ny // 2
-        for d in range(1, half + 1):
-            behind = (y - sign * d + ny) % ny
-            ahead = (y + sign * d + ny) % ny
-            if d < half:
-                src = xl * ny + behind
-                wait(src)
-                if d < half - 1:
-                    send(src, g_pos, pos)
-            ahead_src = xl * ny + ahead
-            wait(ahead_src)
-            send(ahead_src, g_pair, pair)
-            if d < half:
-                send(ahead_src, g_neg, neg)
-                use(src)
-                far = (1 - xl) * ny + behind
-                wait(far)
-                if d < half - 1:
-                    send(far, g_pos, pos)
-                use(far)
-            use(ahead_src)
-            far = (1 - xl) * ny + ahead
-            wait(far)
-            use(far)
+        wait(mate)
+        send(mate, to_pos2, to_pos)
+        wait(ahead[0])
+        send(ahead[0], to_pair)
+        wait(ahead[1])
+        send(ahead[1], to_neg2, to_neg, to_pair)
+        wait(behind[0])
+        wait(behind[1])
+        send(behind[1], to_pos)
+        for src in (mate, ahead[0], ahead[1], behind[0], behind[1]):
+            use(src)
+        wait(far_behind[1])
+        send(far_behind[1], to_pos)
+        wait(ahead[2])
+        send(ahead[2], to_pair)
+        wait(ahead[3])
+        send(ahead[3], to_pair)
+        for src in (far_behind[1], ahead[2], ahead[3]):
+            use(src)
+        for src in (far_behind[0], far_ahead[0], behind[2], far_ahead[1]):
+            wait(src)
+            use(src)
+        for src in (far_behind[2], far_ahead[2], far_ahead[3]):
+            wait(src)
+            use(src)
         return started
 
     residual = tok[:, pl.ds(pl.multiple_of(head * cols, cols), cols)].astype(F32).T
@@ -469,6 +490,8 @@
             dma((2, n_head)),
             dma((2, n_head)),
             dma((2, n_head)),
+            dma((2, n_head)),
+            dma((2, n_head)),
             dma((2,)),
             dma((2,)),
         ],

time: 117 us -> 105 us (0.90)
  Pallas kernels: 111 us -> 98.9 us
    pallas_call x1, Pallas kernels: 111 us -> 98.9 us  [body(): pl.pallas_call(functools.partial(kernel, n_ctx, n_head), out_shape=jax.Sh...]
where the time goes in v2:
time: 105 us; the launch traced here: 104 us
  Pallas kernels  98.9 us (94%)
  local copies, waits for them, and re-layouts  5.46 us (5%)
    pallas_call x1, Pallas kernels, body(): pl.pallas_call(functools.partial(kernel, n_ctx, n_head), out_shape=jax.Sh...  98.9 us
    unnamed x9, local copies, waits for them, and re-layouts  5.46 us

profile of v2, /device:TPU:1, one launch (start us, length us, event | category | flops | bytes accessed | tf_op | source)
XLA Modules:
  0.0 104.4 jit_solution(17200298570014327011)
XLA Ops:
  0.0 0.0 copy-start
  0.0 1.4 %copy-done = bf16[3,2048,128]{2,1,0:T(8,128)(2,1)S(1)} copy-done((bf16[3,2048,128]{2,1,0:T(8,128)(2,1)S(1)}, bf16[3,2048,128]{2,1,0:T(8,128)(2,1)}, u32[]{:S(2)}) %copy-start) | copy-done | bytes 1572888
  1.4 0.0 copy-start.1
  1.4 1.2 %copy-done.1 = bf16[256,2048]{1,0:T(8,128)(2,1)S(1)} copy-done((bf16[256,2048]{1,0:T(8,128)(2,1)S(1)}, bf16[256,2048]{1,0:T(8,128)(2,1)}, u32[]{:S(2)}) %copy-start.1) | copy-done | bytes 1048600
  2.6 0.0 copy-start.2
  2.6 1.1 %copy-done.2 = bf16[2048,12,16]{0,2,1:T(8,128)(2,1)S(1)} copy-done((bf16[2048,12,16]{0,2,1:T(8,128)(2,1)S(1)}, bf16[2048,12,16]{0,2,1:T(8,128)(2,1)}, u32[]{:S(2)}) %copy-start.2) | copy-done | bytes 786456
  3.8 0.0 copy-start.3
  3.8 1.0 copy-done.3
  4.8 98.9 %layer.1 = f32[128,256]{1,0:T(8,128)S(1)} custom-call(bf16[256,2048]{1,0:T(8,128)(2,1)S(1)} %copy-done.1, bf16[3,2048,128]{2,1,0:T(8,128)(2,1)S(1)} %copy-done, bf16[128,2048]{1,0:T(8,128)(2,1)S(1)} %copy-done.3, bf16[192,2048]{1,0:T(8,128)(2,1)S(1)} %bitcast.7), custom_call_target="tpu_custom_call" | custom-call | flops 2885681152 | bytes 4194304 | tf_op jit(solution)/shard_map/layer/pallas_call | solution.py:448
  103.7 0.7 copy.6
Async XLA Ops:
  0.0 1.4 %copy-start = (bf16[3,2048,128]{2,1,0:T(8,128)(2,1)S(1)}, bf16[3,2048,128]{2,1,0:T(8,128)(2,1)}, u32[]{:S(2)}) copy-start(bf16[3,2048,128]{2,1,0:T(8,128)(2,1)} %wqkv_hbm.1) | copy-start | bytes 4718596
  1.4 1.2 %copy-start.1 = (bf16[256,2048]{1,0:T(8,128)(2,1)S(1)}, bf16[256,2048]{1,0:T(8,128)(2,1)}, u32[]{:S(2)}) copy-start(bf16[256,2048]{1,0:T(8,128)(2,1)} %tok_hbm.1) | copy-start | bytes 3145732
  2.6 1.1 %copy-start.2 = (bf16[2048,12,16]{0,2,1:T(8,128)(2,1)S(1)}, bf16[2048,12,16]{0,2,1:T(8,128)(2,1)}, u32[]{:S(2)}) copy-start(bf16[2048,12,16]{0,2,1:T(8,128)(2,1)} %param.7) | copy-start | bytes 2359300
  3.8 1.0 copy-start.3

commit v3 on v2

--- a/solution.py
+++ b/solution.py
@@ -18,6 +18,10 @@
 
 def nt(a, b):
     return lax.dot_general(a, b, (((1,), (1,)), ((), ())), preferred_element_type=F32)
+
+
+def tn(a, b):
+    return lax.dot_general(a, b, (((0,), (0,)), ((), ())), preferred_element_type=F32)
 
 
 def nn(a, b):
@@ -34,10 +38,8 @@
     out_ref,
     tok,
     wqkv,
-    wout,
     wdec,
-    wout_t,
-    wcol_t,
+    wcol,
     q_raw,
     q_pad,
     kbuf,
@@ -105,10 +107,16 @@
             device_id_type=pl.DeviceIdType.MESH,
         )
 
+    own_cols = pl.ds(pl.multiple_of(head * cols, cols), cols)
     loads = [
         pltpu.make_async_copy(a, b, load_sem.at[i])
         for i, (a, b) in enumerate(
-            ((tok_hbm, tok), (wqkv_hbm, wqkv), (wout_hbm, wout), (wdec_hbm, wdec))
+            (
+                (tok_hbm, tok),
+                (wqkv_hbm, wqkv),
+                (wout_hbm.at[:, own_cols], wcol.at[head]),
+                (wdec_hbm, wdec),
+            )
         )
     ]
     for load in loads:
@@ -134,6 +142,18 @@
 
     greet(((ctx + 1) % n_ctx, head))
     greet(((ctx + n_ctx - 1) % n_ctx, head))
+
+    pl.semaphore_wait(barrier, n_head + 6)
+
+    def w_copy(step):
+        other = (head + step) % n_head
+        return remote(
+            wout_hbm.at[:, pl.ds(pl.multiple_of(other * cols, cols), cols)],
+            wcol.at[head],
+            w_send.at[step],
+            w_recv.at[head],
+            (ctx, other),
+        )
 
     loads[0].wait()
     loads[1].wait()
@@ -143,7 +163,6 @@
     keyvals = nn(x, jnp.concatenate([wqkv[1], wqkv[2]], axis=1)) * r
     kbuf[0] = keyvals[:, :cols].astype(BF16)
     vbuf[0] = keyvals[:, cols:].T.astype(BF16)
-    pl.semaphore_wait(barrier, n_head + 6)
 
     first = []
     for t, device in enumerate((dev_up, dev_down)):
@@ -191,20 +210,6 @@
             forward(j, buf, ssem, rsem).start()
 
     ring = ((kbuf, k_send, k_recv), (vbuf, v_send, v_recv))
-
-    loads[2].wait()
-    wout_t[...] = wout[...].astype(F32).T.astype(BF16)
-    wcol_t[head] = wout_t[pl.ds(pl.multiple_of(head * cols, cols), cols), :]
-
-    def w_copy(step):
-        other = (head + step) % n_head
-        return remote(
-            wout_t.at[pl.ds(pl.multiple_of(other * cols, cols), cols), :],
-            wcol_t.at[head],
-            w_send.at[step],
-            w_recv.at[head],
-            (ctx, other),
-        )
 
     m_ref[...] = jnp.full_like(m_ref, -1e30)
     l_ref[...] = jnp.zeros_like(l_ref)
@@ -222,7 +227,7 @@
         q_pad[1, b * rows : (b + 1) * rows, :] = jnp.where(low, zero, q)
 
     def attend(items, h, part):
-        span = slice(part * 2 * rows, (part + 1) * 2 * rows)
+        span = pl.ds(pl.multiple_of(part * 2 * rows, 2 * rows), 2 * rows)
         queries = q_pad[h, span, :]
         scores = [nt(kbuf[j], queries) for j in items]
         old = m_ref[h : h + 1, span]
@@ -243,6 +248,7 @@
     for i in range(4):
         arrive(1 + i // 2, *ring[i % 2])
         attend((0,), i // 2, i % 2)
+
     w_copy(last).start()
 
     @pl.loop(1, nz // 2)
@@ -259,11 +265,9 @@
 
             attend((first_item, first_item + 1), i // 2, i % 2)
 
-    for i in range(4):
-        attend((last,), i // 2, i % 2)
-
     c_copies = []
-    for step in (2, 1, 3):
+
+    def hand_over(step):
         other = (mine + step) % 4
         span = pl.ds(pl.multiple_of(other * rows, rows), rows)
         for h in range(2):
@@ -271,16 +275,23 @@
             stat_send[other, h : h + 1, :] = m_ref[h : h + 1, span]
             stat_send[other, 2 + h : 3 + h, :] = l_ref[h : h + 1, span]
         device = (z * 4 + other, head)
-        c_copies.append(
-            remote(part_send.at[other], part_recv.at[mine], c_send.at[step], c_recv.at[mine], device)
-        )
-        c_copies.append(
-            remote(
-                stat_send.at[other], stat_recv.at[mine], st_send.at[step], st_recv.at[mine], device
-            )
-        )
-        c_copies[-2].start()
-        c_copies[-1].start()
+        for src, dst, ssem, rsem in (
+            (part_send, part_recv, c_send, c_recv),
+            (stat_send, stat_recv, st_send, st_recv),
+        ):
+            copy = remote(src.at[other], dst.at[mine], ssem.at[step], rsem.at[mine], device)
+            copy.start()
+            c_copies.append(copy)
+
+    attend((last,), 0, 1 - xh)
+    attend((last,), 1, 1 - xh)
+    far_core = 3 - 2 * core
+    near_core = 1 + 2 * core
+    hand_over(2)
+    hand_over(far_core)
+    attend((last,), 0, xh)
+    attend((last,), 1, xh)
+    hand_over(near_core)
 
     @pl.loop(1, last)
     def _(j):
@@ -355,15 +366,16 @@
         use(head)
         wait(mate)
         send(mate, to_pos2, to_pos)
+        wait(behind[0])
         wait(ahead[0])
         send(ahead[0], to_pair)
         wait(ahead[1])
         send(ahead[1], to_neg2, to_neg, to_pair)
-        wait(behind[0])
+        for src in (mate, ahead[0], ahead[1], behind[0]):
+            use(src)
         wait(behind[1])
         send(behind[1], to_pos)
-        for src in (mate, ahead[0], ahead[1], behind[0], behind[1]):
-            use(src)
+        use(behind[1])
         wait(far_behind[1])
         send(far_behind[1], to_pos)
         wait(ahead[2])
@@ -386,13 +398,14 @@
     def _(step):
         other = (head + step) % n_head
         remote(
-            wcol_t.at[other], wcol_t.at[other], w_send.at[step], w_recv.at[other], pos
+            wcol.at[other], wcol.at[other], w_send.at[step], w_recv.at[other], pos
         ).wait_recv()
 
+    loads[2].wait()
     total = [residual]
 
     def project(src):
-        total[0] = total[0] + nn(wcol_t[src], att[src])
+        total[0] = total[0] + tn(wcol[src], att[src])
 
     started = gather(0, att, project)
     hid[head] = total[0].astype(BF16)
@@ -453,9 +466,7 @@
         scratch_shapes=[
             pltpu.VMEM((rows, width), BF16),
             pltpu.VMEM(w_qkv.shape, BF16),
-            pltpu.VMEM(w_out.shape, BF16),
             pltpu.VMEM(wdec_t.shape, BF16),
-            pltpu.VMEM((width, cols), BF16),
             pltpu.VMEM((n_head, cols, cols), BF16),
             pltpu.VMEM((4, rows, cols), BF16),
             pltpu.VMEM((2, 4 * rows, cols), BF16),
@@ -496,7 +507,7 @@
             dma((2,)),
         ],
         compiler_params=pltpu.CompilerParams(
-            collective_id=0, has_side_effects=True, vmem_limit_bytes=48 * 1024 * 1024
+            collective_id=0, has_side_effects=True, vmem_limit_bytes=60 * 1024 * 1024
         ),
         cost_estimate=pl.CostEstimate(flops=flops, bytes_accessed=1 << 22, transcendentals=1 << 23),
         name="layer",

time: 105 us -> 101 us (0.962)
  local copies, waits for them, and re-layouts: 5.46 us -> 1.57 us
    unnamed x9 -> x1, local copies, waits for them, and re-layouts: 5.46 us -> 1.57 us
where the time goes in v3:
time: 101 us; the launch traced here: 100 us
  Pallas kernels  98.9 us (98%)
  local copies, waits for them, and re-layouts  1.57 us (2%)
    pallas_call x1, Pallas kernels, body(): pl.pallas_call(functools.partial(kernel, n_ctx, n_head), out_shape=jax.Sh...  98.9 us

profile of v3, /device:TPU:1, one launch (start us, length us, event | category | flops | bytes accessed | tf_op | source)
XLA Modules:
  0.0 100.4 jit_solution(13236135792076839104)
XLA Ops:
  0.0 98.9 %layer.1 = f32[128,256]{1,0:T(8,128)} custom-call(bf16[256,2048]{1,0:T(8,128)(2,1)} %tok_hbm.1, bf16[3,2048,128]{2,1,0:T(8,128)(2,1)} %wqkv_hbm.1, bf16[128,2048]{1,0:T(8,128)(2,1)} %wout_hbm.1, bf16[192,2048]{1,0:T(8,128)(2,1)} %bitcast.7), custom_call_target="tpu_custom_call" | custom-call | flops 2885681152 | bytes 4194304 | tf_op jit(solution)/shard_map/layer/pallas_call | solution.py:461
  98.9 1.6 %copy.6 = f32[256,8,16]{0,2,1:T(8,128)} copy(f32[256,8,16]{0,2,1:T(8,128)} %bitcast.6) | data formatting | bytes 262144

commit v4 on v3

--- a/solution.py
+++ b/solution.py
@@ -214,20 +214,30 @@
     m_ref[...] = jnp.full_like(m_ref, -1e30)
     l_ref[...] = jnp.zeros_like(l_ref)
     acc[...] = jnp.zeros_like(acc)
-    for step in range(1, 4):
+    far_core = 3 - 2 * core
+    near_core = 1 + 2 * core
+    low = lax.broadcasted_iota(jnp.int32, (rows, cols), 1) < HD
+
+    def queries_from(step):
         other = (mine + step) % 4
         remote(
             q_raw.at[other], q_raw.at[other], q_send.at[step], q_recv.at[other], dev_up
         ).wait_recv()
-    low = lax.broadcasted_iota(jnp.int32, (rows, cols), 1) < HD
-    for b in range(4):
-        q = q_raw[b]
-        zero = jnp.zeros_like(q)
-        q_pad[0, b * rows : (b + 1) * rows, :] = jnp.where(low, q, zero)
-        q_pad[1, b * rows : (b + 1) * rows, :] = jnp.where(low, zero, q)
+
+    def spread_queries(part):
+        for c in range(2):
+            b = part * 2 + c
+            q = q_raw[b]
+            zero = jnp.zeros_like(q)
+            place = pl.ds(pl.multiple_of(b * rows, rows), rows)
+            q_pad[0, place, :] = jnp.where(low, q, zero)
+            q_pad[1, place, :] = jnp.where(low, zero, q)
 
     def attend(items, h, part):
-        span = pl.ds(pl.multiple_of(part * 2 * rows, 2 * rows), 2 * rows)
+        if part is None:
+            span = slice(0, 4 * rows)
+        else:
+            span = pl.ds(pl.multiple_of(part * 2 * rows, 2 * rows), 2 * rows)
         queries = q_pad[h, span, :]
         scores = [nt(kbuf[j], queries) for j in items]
         old = m_ref[h : h + 1, span]
@@ -245,25 +255,45 @@
         l_ref[h : h + 1, span] = total
         acc[h, :, span] = summed
 
-    for i in range(4):
-        arrive(1 + i // 2, *ring[i % 2])
-        attend((0,), i // 2, i % 2)
-
+    queries_from(near_core)
+    spread_queries(xh)
+    for h in range(2):
+        arrive(1, *ring[h])
+        attend((0,), h, xh)
+    for i in range(2):
+        arrive(2, *ring[i])
+    w_copy(1).start()
+    for h in range(2):
+        arrive(3, *ring[h])
+        attend((1, 2), h, xh)
+    for i in range(2):
+        arrive(4, *ring[i])
+    w_copy(2).start()
+    queries_from(2)
+    queries_from(far_core)
+    spread_queries(1 - xh)
+    for h in range(2):
+        attend((0,), h, 1 - xh)
+        arrive(5, *ring[h])
+    for h in range(2):
+        attend((1, 2), h, 1 - xh)
+        arrive(6, *ring[h])
     w_copy(last).start()
 
-    @pl.loop(1, nz // 2)
+    @pl.loop(2, nz // 2)
     def _(hop):
         first_item = 2 * hop - 1
         w_copy(first_item).start()
         w_copy(first_item + 1).start()
         for i in range(4):
-            j = first_item + 2 + i // 2
+            j = first_item + 4 + i // 2
 
             @pl.when(j <= last)
             def _():
                 arrive(j, *ring[i % 2])
 
-            attend((first_item, first_item + 1), i // 2, i % 2)
+            if i % 2:
+                attend((first_item, first_item + 1), i // 2, None)
 
     c_copies = []
 
@@ -285,8 +315,6 @@
 
     attend((last,), 0, 1 - xh)
     attend((last,), 1, 1 - xh)
-    far_core = 3 - 2 * core
-    near_core = 1 + 2 * core
     hand_over(2)
     hand_over(far_core)
     attend((last,), 0, xh)

time: 101 us -> 102 us (level)
  Pallas kernels: 98.9 us -> 101 us
    pallas_call x1, Pallas kernels: 98.9 us -> 101 us  [body(): pl.pallas_call(functools.partial(kernel, n_ctx, n_head), out_shape=jax.Sh...]
where the time goes in v4:
time: 102 us
  Pallas kernels  101 us (99%)
  local copies, waits for them, and re-layouts  1.57 us (2%)
    pallas_call x1, Pallas kernels, body(): pl.pallas_call(functools.partial(kernel, n_ctx, n_head), out_shape=jax.Sh...  101 us

profile of v4, /device:TPU:1, one launch (start us, length us, event | category | flops | bytes accessed | tf_op | source)
XLA Modules:
  0.0 102.3 jit_solution(14778748836406396516)
XLA Ops:
  0.0 100.7 %layer.1 = f32[128,256]{1,0:T(8,128)} custom-call(bf16[256,2048]{1,0:T(8,128)(2,1)} %tok_hbm.1, bf16[3,2048,128]{2,1,0:T(8,128)(2,1)} %wqkv_hbm.1, bf16[128,2048]{1,0:T(8,128)(2,1)} %wout_hbm.1, bf16[192,2048]{1,0:T(8,128)(2,1)} %bitcast.7), custom_call_target="tpu_custom_call" | custom-call | flops 2885681152 | bytes 4194304 | tf_op jit(solution)/shard_map/layer/pallas_call | solution.py:489
  100.7 1.6 %copy.6 = f32[256,8,16]{0,2,1:T(8,128)} copy(f32[256,8,16]{0,2,1:T(8,128)} %bitcast.6) | data formatting | bytes 262144
